TPU v7x, 32 devices: a whole 2x2x4 slice. The times are simulated.
32 devices in a mesh: batch: 8 (over y, x, core), chan: 4 (over z).
Axes of the slice: x: 2, y: 2, z: 4, core: 2. Of those that a mesh axis runs over, the one named last changes fastest.
Arguments:
- fine_inputs: bfloat16 [8, 32, 32, 512], P('batch'), may hold values from -6 to 6
- fine_upstream: bfloat16 [8, 32, 32, 512], P('batch', None, None, 'chan'), may hold values from -6 to 6
- fine_bank: bfloat16 [8, 9, 512, 512], P(None, None, 'batch', 'chan'), may hold values from -0.09375 to 0.09375
- fine_coefs: float32 [8, 8], replicated, may hold values from 0 to 1, as said below
- coarse_inputs: bfloat16 [8, 16, 16, 512], P('batch'), may hold values from -6 to 6
- coarse_upstream: bfloat16 [8, 16, 16, 512], P('batch', None, None, 'chan'), may hold values from -6 to 6
- coarse_bank: bfloat16 [8, 9, 512, 512], P(None, None, 'batch', 'chan'), may hold values from -0.09375 to 0.09375
- coarse_coefs: float32 [8, 8], replicated, may hold values from 0 to 1, as said below
Outputs:
- fine_delta: bfloat16 [8, 32, 32, 512], P('batch', None, None, 'chan')
- fine_update: float32 [8, 9, 512, 512], P(None, None, 'batch', 'chan')
- fine_logit: float32 [8, 8], P('batch')
- coarse_delta: bfloat16 [8, 16, 16, 512], P('batch', None, None, 'chan')
- coarse_update: float32 [8, 9, 512, 512], P(None, None, 'batch', 'chan')
- coarse_logit: float32 [8, 8], P('batch')
Inputs may be any that keep to these rules, and one draw needn't show every extreme that they name: Each row of fine_coefs is a softmax: positive entries that sum to one. Each row of coarse_coefs is a softmax: positive entries that sum to one.
All inputs are finite; a program needn't handle non-finite values.
Results may differ from a plain program's by a relative error of at most 0.01.
Values may be sent and summed in bfloat16 or wider, within the bound.
No kernel may reach another device: no remote copies, remote signals or barrier semaphores. Data moves between devices by JAX's collectives and lax.ppermute only.
A program may use at most 128 MiB of HBM per device.

v0:
```python
import jax
import jax.numpy as jnp
from jax import lax
from jax.sharding import PartitionSpec as P

BANKS = 8
FINE_SIDE = 32
COARSE_SIDE = 16
HIGH = lax.Precision.HIGHEST


def shifted(padded, row_shift, col_shift, side):
    window = padded[:, row_shift : row_shift + side, col_shift : col_shift + side, :]
    return window.reshape(window.shape[0], side * side, window.shape[3])


def local_grads(inputs, upstream, kernels, side):
    samples_here = inputs.shape[0]
    pad_in = jnp.pad(inputs, ((0, 0), (1, 1), (1, 1), (0, 0)))
    pad_up = jnp.pad(upstream, ((0, 0), (1, 1), (1, 1), (0, 0)))
    flat_up = upstream.reshape(samples_here, side * side, upstream.shape[3])
    delta = jnp.zeros((samples_here, side * side, inputs.shape[3]), jnp.float32)
    grad_taps = []
    for row_shift in range(3):
        for col_shift in range(3):
            tap = 3 * row_shift + col_shift
            window_in = shifted(pad_in, row_shift, col_shift, side)
            window_up = shifted(pad_up, 2 - row_shift, 2 - col_shift, side)
            grad_taps.append(
                jnp.einsum("bpc,bpo->bco", window_in, flat_up, preferred_element_type=jnp.float32)
                / side
            )
            delta = delta + jnp.einsum(
                "bpo,bco->bpc", window_up, kernels[:, tap], preferred_element_type=jnp.float32
            )
    return (delta.reshape(samples_here, side, side, inputs.shape[3]), jnp.stack(grad_taps, axis=1))


def one_layer(inputs, upstream, bank_part, coefs, side):
    flat_bank = bank_part.reshape(BANKS, -1).astype(jnp.float32)
    mixed_all = jnp.dot(coefs, flat_bank, precision=HIGH)
    mixed_all = mixed_all.reshape((coefs.shape[0],) + bank_part.shape[1:]).astype(jnp.bfloat16)
    kernels = lax.all_to_all(mixed_all, "batch", split_axis=0, concat_axis=2, tiled=True)
    delta, kernel_grad = local_grads(inputs, upstream, kernels, side)
    delta_total = lax.psum(delta.astype(jnp.bfloat16), "chan").astype(jnp.float32)
    width = delta.shape[3] // lax.axis_size("chan")
    delta_part = lax.dynamic_slice_in_dim(delta_total, lax.axis_index("chan") * width, width, 3)
    moved = lax.all_to_all(
        kernel_grad.astype(jnp.bfloat16), "batch", split_axis=2, concat_axis=0, tiled=True
    ).astype(kernel_grad.dtype)
    flat_grads = moved.reshape(moved.shape[0], -1)
    update = jnp.dot(coefs.T, flat_grads, precision=HIGH).reshape(bank_part.shape)
    dcoef_part = lax.dot_general(flat_grads, flat_bank, (((1,), (1,)), ((), ())), precision=HIGH)
    return (delta_part.astype(jnp.bfloat16), update, dcoef_part)


def logit_grads(coefs, totals, samples_here):
    first_row = lax.axis_index("batch") * samples_here
    own_coefs = lax.dynamic_slice_in_dim(coefs, first_row, samples_here, 0)
    own_totals = lax.dynamic_slice_in_dim(totals, first_row, samples_here, 0)
    return own_coefs * (own_totals - jnp.sum(own_coefs * own_totals, axis=1, keepdims=True))


def per_device(
    fine_inputs,
    fine_upstream,
    fine_bank,
    fine_coefs,
    coarse_inputs,
    coarse_upstream,
    coarse_bank,
    coarse_coefs,
):
    fine_delta, fine_update, fine_partial = one_layer(
        fine_inputs, fine_upstream, fine_bank, fine_coefs, FINE_SIDE
    )
    coarse_delta, coarse_update, coarse_partial = one_layer(
        coarse_inputs, coarse_upstream, coarse_bank, coarse_coefs, COARSE_SIDE
    )
    fine_total, coarse_total = lax.psum((fine_partial, coarse_partial), ("batch", "chan"))
    samples_here = fine_inputs.shape[0]
    fine_logit = logit_grads(fine_coefs, fine_total, samples_here)
    coarse_logit = logit_grads(coarse_coefs, coarse_total, samples_here)
    return (fine_delta, fine_update, fine_logit, coarse_delta, coarse_update, coarse_logit)


def solution(mesh):
    return jax.shard_map(
        per_device,
        mesh=mesh,
        in_specs=(
            P("batch", None, None, None),
            P("batch", None, None, "chan"),
            P(None, None, "batch", "chan"),
            P(),
            P("batch", None, None, None),
            P("batch", None, None, "chan"),
            P(None, None, "batch", "chan"),
            P(),
        ),
        out_specs=(
            P("batch", None, None, "chan"),
            P(None, None, "batch", "chan"),
            P("batch", None),
            P("batch", None, None, "chan"),
            P(None, None, "batch", "chan"),
            P("batch", None),
        ),
        check_vma=False,
    )
```

profile of v0, /device:TPU:10, one launch (start us, length us, event | category | flops | bytes accessed | tf_op | source)
XLA Modules:
  0.0 182.0 jit_solution(2190526697358805732)
XLA Ops:
  7.2 2.0 %copy.47 = bf16[1,8,576,128]{3,1,2,0:T(8,128)(2,1)S(1)} copy(bf16[1,8,576,128]{3,2,1,0:T(8,128)(2,1)} %bitcast.542) | data formatting | bytes 2359296
  9.2 1.1 convolution_convert_fusion.1
  10.3 1.3 copy.24
  11.6 4.4 %all-to-all-start = ((bf16[8,9,64,128]{3,2,1,0:T(8,128)(2,1)}), bf16[8,9,64,128]{3,2,1,0:T(8,128)(2,1)S(1)}, u32[]{:S(2)}, u32[]{:S(2)}) async-start(bf16[8,9,64,128]{3,2,1,0:T(8,128)(2,1)} %copy.24), calls=%async_computation | async-start | bytes 2359296 | tf_op jit(solution)/shard_map/all_to_all | solution.py:43
  16.0 0.8 copy.46
  17.0 0.4 copy-done.22
  17.3 0.5 fusion.78
  17.8 0.5 fusion.76
  18.4 0.6 fusion.74
  18.9 0.6 fusion.72
  19.5 0.5 fusion.70
  20.0 0.5 fusion.68
  20.6 0.6 fusion.66
  21.2 0.6 fusion.64
  21.7 0.6 fusion.62
  23.3 0.3 fusion.56
  23.6 0.3 fusion.54
  24.2 0.4 copy-done.21
  24.5 1.1 convolution_convert_fusion
  25.9 1.3 copy.29
  27.2 2.2 %copy.27 = bf16[1,9,512,128]{3,1,0,2:T(8,128)(2,1)} copy(bf16[1,9,512,128]{3,2,1,0:T(8,128)(2,1)S(1)} %fusion.62) | data formatting | bytes 2359296 | tf_op jit(solution)/shard_map/stack | solution.py:36
  29.5 1.3 fusion.48
  31.1 0.3 fusion.44
  31.4 2.2 %copy.31 = bf16[1,9,512,128]{3,1,0,2:T(8,128)(2,1)} copy(bf16[1,9,512,128]{3,2,1,0:T(8,128)(2,1)S(1)} %fusion.44) | data formatting | bytes 2359296 | tf_op jit(solution)/shard_map/stack | solution.py:36
  33.6 0.8 pad_slice_fusion.24
  34.4 1.2 pad_slice_fusion.16
  35.6 4.3 %all-to-all-start.1 = ((bf16[1,9,512,128]{3,1,0,2:T(8,128)(2,1)}), bf16[1,9,512,128]{3,1,0,2:T(8,128)(2,1)}, u32[]{:S(2)}, u32[]{:S(2)}) async-start(bf16[1,9,512,128]{3,1,0,2:T(8,128)(2,1)} %copy.27), calls=%async_computation.1 | async-start | bytes 4194304 | tf_op jit(solution)/shard_map/all_to_all | solution.py:48
  40.0 0.4 fusion.123
  40.5 1.8 fusion.124
  42.2 1.7 fusion.125
  44.0 1.7 fusion.126
  45.7 19.4 %all-to-all-done.1 = bf16[1,9,512,128]{3,1,0,2:T(8,128)(2,1)} async-done(((bf16[1,9,512,128]{3,1,0,2:T(8,128)(2,1)}), bf16[1,9,512,128]{3,1,0,2:T(8,128)(2,1)}, u32[]{:S(2)}, u32[]{:S(2)}) %all-to-all-start.1) | async-done | bytes 1179680 | tf_op jit(solution)/shard_map/all_to_all | solution.py:48
  65.1 5.7 %all-to-all-start.2 = ((bf16[8,9,64,128]{3,2,1,0:T(8,128)(2,1)}), bf16[8,9,64,128]{3,2,1,0:T(8,128)(2,1)}, u32[]{:S(2)}, u32[]{:S(2)}) async-start(bf16[8,9,64,128]{3,2,1,0:T(8,128)(2,1)} %copy.29), calls=%async_computation.2 | async-start | bytes 2359296 | tf_op jit(solution)/shard_map/all_to_all | solution.py:43
  70.8 3.0 %copy.49 = bf16[1,9,8,64,128]{4,3,1,2,0:T(8,128)(2,1)} copy(bf16[1,9,8,64,128]{4,1,3,2,0:T(8,128)(2,1)} %bitcast.57) | data formatting | bytes 2359296 | tf_op jit(solution)/shard_map/all_to_all | solution.py:48
  73.8 1.8 reshape.837
  75.5 2.9 %fusion.127 = f32[1024,512]{1,0:T(8,128)} fusion(bf16[1024,128]{1,0:T(8,128)(2,1)} %bitcast.554, bf16[1,9,512,128]{3,2,1,0:T(8,128)(2,1)} %bitcast.526), kind=kOutput, calls=%fused_computation.192 | convolution fusion | flops 134217728 | bytes 2490368 | tf_op jit(solution)/shard_map/bpo,bco->bpc/dot_general | solution.py:33
  78.4 2.7 %fusion.128 = f32[1024,512]{1,0:T(8,128)} fusion(bf16[1024,128]{1,0:T(8,128)(2,1)S(1)} %bitcast.553, bf16[1,9,512,128]{3,2,1,0:T(8,128)(2,1)} %bitcast.527), kind=kOutput, calls=%fused_computation.194 | convolution fusion | flops 134217728 | bytes 2490368 | tf_op jit(solution)/shard_map/bpo,bco->bpc/dot_general | solution.py:33
  81.1 2.7 %fusion.130 = f32[1024,512]{1,0:T(8,128)} fusion(bf16[1024,128]{1,0:T(8,128)(2,1)S(1)} %bitcast.552, bf16[1,9,512,128]{3,2,1,0:T(8,128)(2,1)} %bitcast.528), kind=kOutput, calls=%fused_computation.198 | convolution fusion | flops 134217728 | bytes 2490368 | tf_op jit(solution)/shard_map/bpo,bco->bpc/dot_general | solution.py:33
  83.8 2.7 %fusion.129 = f32[1024,512]{1,0:T(8,128)} fusion(bf16[1024,128]{1,0:T(8,128)(2,1)S(1)} %bitcast.551, bf16[1,9,512,128]{3,2,1,0:T(8,128)(2,1)} %bitcast.529), kind=kOutput, calls=%fused_computation.196 | convolution fusion | flops 134217728 | bytes 2490368 | tf_op jit(solution)/shard_map/bpo,bco->bpc/dot_general | solution.py:33
  86.5 5.4 %all-to-all-start.3 = ((bf16[1,9,512,128]{3,1,0,2:T(8,128)(2,1)}), bf16[1,9,512,128]{3,1,0,2:T(8,128)(2,1)}, u32[]{:S(2)}, u32[]{:S(2)}) async-start(bf16[1,9,512,128]{3,1,0,2:T(8,128)(2,1)} %copy.31), calls=%async_computation.3 | async-start | bytes 4194304 | tf_op jit(solution)/shard_map/all_to_all | solution.py:48
  91.9 1.5 copy.30
  93.5 1.1 fusion.122
  94.6 1.1 convolution_add_fusion.6
  95.8 1.2 convolution_add_fusion.5
  97.0 1.2 convolution_add_fusion.4
  98.5 1.2 convolution_add_fusion.3
  100.2 1.9 %fusion.6 = bf16[256,512]{1,0:T(8,128)(2,1)} fusion(f32[256,512]{1,0:T(8,128)S(1)} %convolution_add_fusion.1, bf16[256,128]{1,0:T(8,128)(2,1)} %bitcast.567, bf16[1,9,512,128]{3,2,1,0:T(8,128)(2,1)S(1)} %bitcast.539), kind=kOutput, calls=%fused_computation.25 | convolution fusion | flops 33816576 | bytes 983040 | tf_op jit(solution)/shard_map/bpo,bco->bpc/dot_general | solution.py:33
  102.2 3.8 %fusion.4 = bf16[1024,512]{1,0:T(8,128)(2,1)} fusion(f32[1024,512]{1,0:T(8,128)S(1)} %fusion.123, f32[1024,512]{1,0:T(8,128)S(1)} %copy-done, f32[1024,512]{1,0:T(8,128)S(1)} %copy-done.1, f32[512,1024]{0,1:T(8,128)S(1)} %copy-done.2, f32[1024,512]{1,0:T(8,128)S(1)} %copy-done.3, f32[1024,512]{1,0:T(8,128)S(1)} %copy-done.4, f32[1024,512]{1,0:T(8,128)S(1)} %copy-done.5, ...), kind=kOutput, calls=%fused_computation.5 | convolution fusion | flops 138936320 | bytes 18219008 | tf_op jit(solution)/shard_map/bpo,bco->bpc/dot_general | solution.py:33
  106.0 1.2 fusion.160
  107.2 1.8 %copy.33 = f32[8,9,64,128]{3,2,1,0:T(8,128)} copy(f32[8,9,64,128]{3,0,2,1:T(8,128)S(1)} %bitcast.520) | data formatting | bytes 4718592
  109.0 8.1 %all-to-all-done.3 = bf16[1,9,512,128]{3,1,0,2:T(8,128)(2,1)} async-done(((bf16[1,9,512,128]{3,1,0,2:T(8,128)(2,1)}), bf16[1,9,512,128]{3,1,0,2:T(8,128)(2,1)}, u32[]{:S(2)}, u32[]{:S(2)}) %all-to-all-start.3) | async-done | bytes 1179680 | tf_op jit(solution)/shard_map/all_to_all | solution.py:48
  117.2 1.9 %copy.48 = bf16[1,9,8,64,128]{4,3,1,2,0:T(8,128)(2,1)S(1)} copy(bf16[1,9,8,64,128]{4,1,3,2,0:T(8,128)(2,1)} %bitcast.118) | data formatting | bytes 2359296 | tf_op jit(solution)/shard_map/all_to_all | solution.py:48
  119.1 0.5 reshape.868
  119.6 1.2 fusion.161
  120.8 1.8 %copy.34 = f32[8,9,64,128]{3,2,1,0:T(8,128)} copy(f32[8,9,64,128]{3,0,2,1:T(8,128)S(1)} %bitcast.521) | data formatting | bytes 4718592
  122.6 1.1 fusion.158
  123.9 1.1 fusion.159
  125.0 43.5 %all-reduce.4 = (f32[8,8]{1,0:T(8,128)S(1)}, f32[8,8]{1,0:T(8,128)S(1)}) all-reduce(f32[8,8]{1,0:T(8,128)S(1)} %fusion.158, f32[8,8]{1,0:T(8,128)S(1)} %fusion.159), channel_id=1, replica_groups=mesh['batch'=8,'chan'=4] {'batch','chan'}, use_global_device_ids=true, to_apply=%region_1.2 | all-reduce | flops 128 | bytes 1024 | tf_op jit(solution)/shard_map/psum | solution.py:80
  168.4 0.6 multiply_reduce_fusion.1
  169.0 0.6 multiply_reduce_fusion
  169.6 1.2 subtract_multiply_fusion.1
  170.8 1.2 subtract_multiply_fusion
  172.0 1.7 convert_convert_fusion
  173.6 1.5 convert_convert_fusion.1
  (62 shorter events, 3.1 us)
Async XLA Ops:
  7.2 2.1 %copy-start.20 = (f32[8,8]{1,0:T(8,128)S(1)}, f32[8,8]{1,0:T(8,128)}, u32[]{:S(2)}) copy-start(f32[8,8]{1,0:T(8,128)} %param.11) | copy-start | bytes 772
  11.6 4.4 %copy-start.8 = (bf16[8,9,64,128]{3,2,1,0:T(8,128)(2,1)S(1)}, bf16[8,9,64,128]{3,2,1,0:T(8,128)(2,1)}, u32[]{:S(2)}) copy-start(bf16[8,9,64,128]{3,2,1,0:T(8,128)(2,1)} %param.14) | copy-start | bytes 3538948
  11.6 24.0 %all-to-all-start = ((bf16[8,9,64,128]{3,2,1,0:T(8,128)(2,1)}), bf16[8,9,64,128]{3,2,1,0:T(8,128)(2,1)S(1)}, u32[]{:S(2)}, u32[]{:S(2)}) async-start(bf16[8,9,64,128]{3,2,1,0:T(8,128)(2,1)} %copy.24), calls=%async_computation | async-start | bytes 2359296 | tf_op jit(solution)/shard_map/all_to_all | solution.py:43
  16.0 1.0 copy-start.10
  16.0 1.3 copy-start.22
  21.7 0.8 copy-start.15
  21.7 1.0 copy-start.23
  23.9 0.7 copy-start.21
  29.5 1.3 copy-start.16
  29.5 1.3 copy-start.24
  31.4 3.0 %copy-start.11 = (bf16[1,32,32,128]{3,2,1,0:T(8,128)(2,1)S(1)}, bf16[1,32,32,128]{3,2,1,0:T(8,128)(2,1)}, u32[]{:S(2)}) copy-start(bf16[1,32,32,128]{3,2,1,0:T(8,128)(2,1)} %param.9) | copy-start | bytes 786436
  35.6 29.5 %all-to-all-start.1 = ((bf16[1,9,512,128]{3,1,0,2:T(8,128)(2,1)}), bf16[1,9,512,128]{3,1,0,2:T(8,128)(2,1)}, u32[]{:S(2)}, u32[]{:S(2)}) async-start(bf16[1,9,512,128]{3,1,0,2:T(8,128)(2,1)} %copy.27), calls=%async_computation.1 | async-start | bytes 4194304 | tf_op jit(solution)/shard_map/all_to_all | solution.py:48
  40.0 4.0 %copy-start.6 = (bf16[8,9,64,128]{3,2,0,1:T(8,128)(2,1)}, bf16[8,9,64,128]{3,2,0,1:T(8,128)(2,1)S(1)}, u32[]{:S(2)}) copy-start(bf16[8,9,64,128]{3,2,0,1:T(8,128)(2,1)S(1)} %copy.25) | copy-start | bytes 3538948
  65.1 21.4 %all-to-all-start.2 = ((bf16[8,9,64,128]{3,2,1,0:T(8,128)(2,1)}), bf16[8,9,64,128]{3,2,1,0:T(8,128)(2,1)}, u32[]{:S(2)}, u32[]{:S(2)}) async-start(bf16[8,9,64,128]{3,2,1,0:T(8,128)(2,1)} %copy.29), calls=%async_computation.2 | async-start | bytes 2359296 | tf_op jit(solution)/shard_map/all_to_all | solution.py:43
  75.5 2.9 %copy-start.14 = (bf16[1,32,32,128]{3,2,1,0:T(8,128)(2,1)S(1)}, bf16[1,32,32,128]{3,2,1,0:T(8,128)(2,1)}, u32[]{:S(2)}) copy-start(bf16[1,32,32,128]{3,2,1,0:T(8,128)(2,1)} %get-tuple-element.30) | copy-start | bytes 786436
  78.4 2.7 %copy-start.13 = (bf16[1,32,32,128]{3,2,1,0:T(8,128)(2,1)S(1)}, bf16[1,32,32,128]{3,2,1,0:T(8,128)(2,1)}, u32[]{:S(2)}) copy-start(bf16[1,32,32,128]{3,2,1,0:T(8,128)(2,1)} %get-tuple-element.35) | copy-start | bytes 786436
  81.1 2.7 %copy-start.12 = (bf16[1,32,32,128]{3,2,1,0:T(8,128)(2,1)S(1)}, bf16[1,32,32,128]{3,2,1,0:T(8,128)(2,1)}, u32[]{:S(2)}) copy-start(bf16[1,32,32,128]{3,2,1,0:T(8,128)(2,1)} %get-tuple-element.29) | copy-start | bytes 786436
  86.5 30.6 %all-to-all-start.3 = ((bf16[1,9,512,128]{3,1,0,2:T(8,128)(2,1)}), bf16[1,9,512,128]{3,1,0,2:T(8,128)(2,1)}, u32[]{:S(2)}, u32[]{:S(2)}) async-start(bf16[1,9,512,128]{3,1,0,2:T(8,128)(2,1)} %copy.31), calls=%async_computation.3 | async-start | bytes 4194304 | tf_op jit(solution)/shard_map/all_to_all | solution.py:48
  91.9 80.0 %all-reduce.8.cloned.1.call-start = ((), (), s32[]{:S(2)}) async-start(), calls=%async_computation.4 | async-start | bytes 2621440 | tf_op jit(solution)/shard_map/psum | solution.py:45
  91.9 10.2 %copy-start.4 = (f32[1024,512]{1,0:T(8,128)S(1)}, f32[1024,512]{1,0:T(8,128)}, u32[]{:S(2)}) copy-start(f32[1024,512]{1,0:T(8,128)} %fusion.128) | copy-start | bytes 6291460
  91.9 10.2 %copy-start.5 = (f32[1024,512]{1,0:T(8,128)S(1)}, f32[1024,512]{1,0:T(8,128)}, u32[]{:S(2)}) copy-start(f32[1024,512]{1,0:T(8,128)} %fusion.130) | copy-start | bytes 6291460
  94.6 5.1 %copy-start.19 = (bf16[1,16,16,128]{3,2,1,0:T(8,128)(2,1)S(1)}, bf16[1,16,16,128]{3,2,1,0:T(8,128)(2,1)}, u32[]{:S(2)}) copy-start(bf16[1,16,16,128]{3,2,1,0:T(8,128)(2,1)} %get-tuple-element.41) | copy-start | bytes 196612
  94.6 5.4 %copy-start.18 = (bf16[1,16,16,128]{3,2,1,0:T(8,128)(2,1)S(1)}, bf16[1,16,16,128]{3,2,1,0:T(8,128)(2,1)}, u32[]{:S(2)}) copy-start(bf16[1,16,16,128]{3,2,1,0:T(8,128)(2,1)} %get-tuple-element.42) | copy-start | bytes 196612
  95.7 2.5 %copy-start.17 = (bf16[1,16,16,128]{3,2,1,0:T(8,128)(2,1)S(1)}, bf16[1,16,16,128]{3,2,1,0:T(8,128)(2,1)}, u32[]{:S(2)}) copy-start(bf16[1,16,16,128]{3,2,1,0:T(8,128)(2,1)} %param.13) | copy-start | bytes 196612
  95.8 6.4 %copy-start.3 = (f32[1024,512]{1,0:T(8,128)S(1)}, f32[1024,512]{1,0:T(8,128)}, u32[]{:S(2)}) copy-start(f32[1024,512]{1,0:T(8,128)} %fusion.127) | copy-start | bytes 6291460
  97.0 5.2 %copy-start.2 = (f32[512,1024]{0,1:T(8,128)S(1)}, f32[512,1024]{0,1:T(8,128)}, u32[]{:S(2)}) copy-start(f32[512,1024]{0,1:T(8,128)} %fusion.126) | copy-start | bytes 6291460
  98.5 3.7 %copy-start.1 = (f32[1024,512]{1,0:T(8,128)S(1)}, f32[1024,512]{1,0:T(8,128)}, u32[]{:S(2)}) copy-start(f32[1024,512]{1,0:T(8,128)} %fusion.125) | copy-start | bytes 6291460
  100.0 2.2 %copy-start = (f32[1024,512]{1,0:T(8,128)S(1)}, f32[1024,512]{1,0:T(8,128)}, u32[]{:S(2)}) copy-start(f32[1024,512]{1,0:T(8,128)} %fusion.124) | copy-start | bytes 6291460
  120.8 1.8 %copy-start.7 = (bf16[8,9,64,128]{3,2,1,0:T(8,128)(2,1)S(1)}, bf16[8,9,64,128]{3,2,1,0:T(8,128)(2,1)}, u32[]{:S(2)}) copy-start(bf16[8,9,64,128]{3,2,1,0:T(8,128)(2,1)} %param.10) | copy-start | bytes 3538948
  122.6 1.3 copy-start.9
Sparse Core Ops, SparseCore 0:
  106.1 61.7 all-reduce.7
where the time goes:
time: 183 us; the launch traced here: 182 us
  matrix products  44.1 us (24%)
  blocking collectives  43.5 us (24%)
  waiting for transfers between devices  27.5 us (15%)
  local copies, waits for them, and re-layouts  26 us (14%)
  starting transfers between devices  19.8 us (11%)
  between operations  14.5 us (8%)
  other arithmetic  6.68 us (4%)
    psum x1, blocking collectives, per_device(): lax.psum((fine_partial, coarse_partial), ('batch', 'chan'))  43.5 us
    dot_general x18, matrix products, local_grads(): jnp.einsum('bpo,bco->bpc', window_up, kernels[:, tap], preferred_element_...  29 us
    all_to_all x2, waiting for transfers between devices, one_layer(): lax.all_to_all(kernel_grad.astype(jnp.bfloat16), 'batch', split_axis=2, c...  27.5 us
    all_to_all x2, starting transfers between devices, one_layer(): lax.all_to_all(mixed_all, 'batch', split_axis=0, concat_axis=2, tiled=True)  10 us
    all_to_all x2, starting transfers between devices, one_layer(): lax.all_to_all(kernel_grad.astype(jnp.bfloat16), 'batch', split_axis=2, c...  9.71 us
    dot_general x18, matrix products, local_grads(): jnp.einsum('bpc,bpo->bco', window_in, flat_up, preferred_element_type=jnp...  8.47 us
    unnamed x54, local copies, waits for them, and re-layouts  8.13 us
    all_to_all x2, local copies, waits for them, and re-layouts, one_layer(): lax.all_to_all(kernel_grad.astype(jnp.bfloat16), 'batch', split_axis=2, c...  4.92 us
  transfers between devices with their start and end apart: 5, of which 2 were waited for; matrix products, arithmetic and copies ran while one was open for 37% of the time, Pallas kernels for 0%

commit v1 on v0

--- a/solution.py
+++ b/solution.py
@@ -77,7 +77,7 @@
     coarse_delta, coarse_update, coarse_partial = one_layer(
         coarse_inputs, coarse_upstream, coarse_bank, coarse_coefs, COARSE_SIDE
     )
-    fine_total, coarse_total = lax.psum((fine_partial, coarse_partial), ("batch", "chan"))
+    fine_total, coarse_total = lax.psum(lax.psum((fine_partial, coarse_partial), "chan"), "batch")
     samples_here = fine_inputs.shape[0]
     fine_logit = logit_grads(fine_coefs, fine_total, samples_here)
     coarse_logit = logit_grads(coarse_coefs, coarse_total, samples_here)

time: 183 us -> 181 us (0.989); the launches traced: 182 us -> 178 us
  blocking collectives: 43.5 us -> 20 us
  waiting for transfers between devices: 27.5 us -> 46.9 us
    psum x1 -> x2, blocking collectives: 43.5 us -> 20 us  [the longest x1 10.3 us: per_device(): lax.psum(lax.psum((fine_partial, coarse_partial), 'chan'), 'batch')]
    psum x1, waiting for transfers between devices: 0.01 us -> 19.4 us  [one_layer(): lax.psum(delta.astype(jnp.bfloat16), 'chan').astype(jnp.float32)]
  transfers between devices with their start and end apart: 5 -> 5, of which waited for: 2 -> 3; matrix products, arithmetic and copies ran while one was open for 37% -> 38% of each run, Pallas kernels for 0% -> 0%
where the time goes in v1:
time: 181 us; the launch traced here: 178 us
  waiting for transfers between devices  46.9 us (26%)
  matrix products  44.1 us (24%)
  local copies, waits for them, and re-layouts  26 us (14%)
  blocking collectives  20 us (11%)
  starting transfers between devices  19.7 us (11%)
  between operations  14.5 us (8%)
  other arithmetic  6.68 us (4%)
    dot_general x18, matrix products, local_grads(): jnp.einsum('bpo,bco->bpc', window_up, kernels[:, tap], preferred_element_...  29 us
    all_to_all x2, waiting for transfers between devices, one_layer(): lax.all_to_all(kernel_grad.astype(jnp.bfloat16), 'batch', split_axis=2, c...  27.5 us
    psum x1, waiting for transfers between devices, one_layer(): lax.psum(delta.astype(jnp.bfloat16), 'chan').astype(jnp.float32)  19.4 us
    psum x1, blocking collectives, per_device(): lax.psum(lax.psum((fine_partial, coarse_partial), 'chan'), 'batch')  10.3 us
    all_to_all x2, starting transfers between devices, one_layer(): lax.all_to_all(mixed_all, 'batch', split_axis=0, concat_axis=2, tiled=True)  10 us
    all_to_all x2, starting transfers between devices, one_layer(): lax.all_to_all(kernel_grad.astype(jnp.bfloat16), 'batch', split_axis=2, c...  9.7 us
    psum x1, blocking collectives, per_device(): lax.psum((fine_partial, coarse_partial), 'chan')  9.69 us
    dot_general x18, matrix products, local_grads(): jnp.einsum('bpc,bpo->bco', window_in, flat_up, preferred_element_type=jnp...  8.47 us
  transfers between devices with their start and end apart: 5, of which 3 were waited for; matrix products, arithmetic and copies ran while one was open for 38% of the time, Pallas kernels for 0%

profile of v1, /device:TPU:10, one launch (start us, length us, event | category | flops | bytes accessed | tf_op | source)
XLA Modules:
  0.0 177.9 jit_solution(14856702704978234312)
XLA Ops:
  7.2 2.0 %copy.47 = bf16[1,8,576,128]{3,1,2,0:T(8,128)(2,1)S(1)} copy(bf16[1,8,576,128]{3,2,1,0:T(8,128)(2,1)} %bitcast.542) | data formatting | bytes 2359296
  9.2 1.1 convolution_convert_fusion.1
  10.3 1.3 copy.24
  11.6 4.4 %all-to-all-start = ((bf16[8,9,64,128]{3,2,1,0:T(8,128)(2,1)}), bf16[8,9,64,128]{3,2,1,0:T(8,128)(2,1)S(1)}, u32[]{:S(2)}, u32[]{:S(2)}) async-start(bf16[8,9,64,128]{3,2,1,0:T(8,128)(2,1)} %copy.24), calls=%async_computation | async-start | bytes 2359296 | tf_op jit(solution)/shard_map/all_to_all | solution.py:43
  16.0 0.8 copy.46
  17.0 0.4 copy-done.22
  17.3 0.5 fusion.78
  17.8 0.5 fusion.76
  18.4 0.6 fusion.74
  18.9 0.6 fusion.72
  19.5 0.5 fusion.70
  20.0 0.5 fusion.68
  20.6 0.6 fusion.66
  21.2 0.6 fusion.64
  21.7 0.6 fusion.62
  24.2 0.4 copy-done.21
  24.5 1.1 convolution_convert_fusion
  25.9 1.3 copy.29
  27.3 2.2 %copy.27 = bf16[1,9,512,128]{3,1,0,2:T(8,128)(2,1)} copy(bf16[1,9,512,128]{3,2,1,0:T(8,128)(2,1)S(1)} %fusion.62) | data formatting | bytes 2359296 | tf_op jit(solution)/shard_map/stack | solution.py:36
  29.5 1.3 fusion.48
  31.1 0.3 fusion.44
  31.4 2.2 %copy.31 = bf16[1,9,512,128]{3,1,0,2:T(8,128)(2,1)} copy(bf16[1,9,512,128]{3,2,1,0:T(8,128)(2,1)S(1)} %fusion.44) | data formatting | bytes 2359296 | tf_op jit(solution)/shard_map/stack | solution.py:36
  33.6 0.8 pad_slice_fusion.24
  34.4 1.2 pad_slice_fusion.16
  35.6 4.3 %all-to-all-start.1 = ((bf16[1,9,512,128]{3,1,0,2:T(8,128)(2,1)}), bf16[1,9,512,128]{3,1,0,2:T(8,128)(2,1)}, u32[]{:S(2)}, u32[]{:S(2)}) async-start(bf16[1,9,512,128]{3,1,0,2:T(8,128)(2,1)} %copy.27), calls=%async_computation.1 | async-start | bytes 4194304 | tf_op jit(solution)/shard_map/all_to_all | solution.py:48
  40.0 0.4 fusion.123
  40.5 1.8 fusion.124
  42.2 1.7 fusion.125
  44.0 1.7 fusion.126
  45.7 19.4 %all-to-all-done.1 = bf16[1,9,512,128]{3,1,0,2:T(8,128)(2,1)} async-done(((bf16[1,9,512,128]{3,1,0,2:T(8,128)(2,1)}), bf16[1,9,512,128]{3,1,0,2:T(8,128)(2,1)}, u32[]{:S(2)}, u32[]{:S(2)}) %all-to-all-start.1) | async-done | bytes 1179680 | tf_op jit(solution)/shard_map/all_to_all | solution.py:48
  65.1 5.7 %all-to-all-start.2 = ((bf16[8,9,64,128]{3,2,1,0:T(8,128)(2,1)}), bf16[8,9,64,128]{3,2,1,0:T(8,128)(2,1)}, u32[]{:S(2)}, u32[]{:S(2)}) async-start(bf16[8,9,64,128]{3,2,1,0:T(8,128)(2,1)} %copy.29), calls=%async_computation.2 | async-start | bytes 2359296 | tf_op jit(solution)/shard_map/all_to_all | solution.py:43
  70.8 3.0 %copy.49 = bf16[1,9,8,64,128]{4,3,1,2,0:T(8,128)(2,1)} copy(bf16[1,9,8,64,128]{4,1,3,2,0:T(8,128)(2,1)} %bitcast.57) | data formatting | bytes 2359296 | tf_op jit(solution)/shard_map/all_to_all | solution.py:48
  73.8 1.8 reshape.837
  75.5 2.9 %fusion.127 = f32[1024,512]{1,0:T(8,128)} fusion(bf16[1024,128]{1,0:T(8,128)(2,1)} %bitcast.554, bf16[1,9,512,128]{3,2,1,0:T(8,128)(2,1)} %bitcast.526), kind=kOutput, calls=%fused_computation.192 | convolution fusion | flops 134217728 | bytes 2490368 | tf_op jit(solution)/shard_map/bpo,bco->bpc/dot_general | solution.py:33
  78.4 2.7 %fusion.128 = f32[1024,512]{1,0:T(8,128)} fusion(bf16[1024,128]{1,0:T(8,128)(2,1)S(1)} %bitcast.553, bf16[1,9,512,128]{3,2,1,0:T(8,128)(2,1)} %bitcast.527), kind=kOutput, calls=%fused_computation.194 | convolution fusion | flops 134217728 | bytes 2490368 | tf_op jit(solution)/shard_map/bpo,bco->bpc/dot_general | solution.py:33
  81.1 2.7 %fusion.130 = f32[1024,512]{1,0:T(8,128)} fusion(bf16[1024,128]{1,0:T(8,128)(2,1)S(1)} %bitcast.552, bf16[1,9,512,128]{3,2,1,0:T(8,128)(2,1)} %bitcast.528), kind=kOutput, calls=%fused_computation.198 | convolution fusion | flops 134217728 | bytes 2490368 | tf_op jit(solution)/shard_map/bpo,bco->bpc/dot_general | solution.py:33
  83.8 2.7 %fusion.129 = f32[1024,512]{1,0:T(8,128)} fusion(bf16[1024,128]{1,0:T(8,128)(2,1)S(1)} %bitcast.551, bf16[1,9,512,128]{3,2,1,0:T(8,128)(2,1)} %bitcast.529), kind=kOutput, calls=%fused_computation.196 | convolution fusion | flops 134217728 | bytes 2490368 | tf_op jit(solution)/shard_map/bpo,bco->bpc/dot_general | solution.py:33
  86.5 5.4 %all-to-all-start.3 = ((bf16[1,9,512,128]{3,1,0,2:T(8,128)(2,1)}), bf16[1,9,512,128]{3,1,0,2:T(8,128)(2,1)}, u32[]{:S(2)}, u32[]{:S(2)}) async-start(bf16[1,9,512,128]{3,1,0,2:T(8,128)(2,1)} %copy.31), calls=%async_computation.3 | async-start | bytes 4194304 | tf_op jit(solution)/shard_map/all_to_all | solution.py:48
  91.9 1.5 copy.30
  93.5 1.1 fusion.122
  94.6 1.1 convolution_add_fusion.6
  95.8 1.2 convolution_add_fusion.5
  97.0 1.2 convolution_add_fusion.4
  98.5 1.2 convolution_add_fusion.3
  100.2 1.9 %fusion.6 = bf16[256,512]{1,0:T(8,128)(2,1)} fusion(f32[256,512]{1,0:T(8,128)S(1)} %convolution_add_fusion.1, bf16[256,128]{1,0:T(8,128)(2,1)} %bitcast.567, bf16[1,9,512,128]{3,2,1,0:T(8,128)(2,1)S(1)} %bitcast.539), kind=kOutput, calls=%fused_computation.25 | convolution fusion | flops 33816576 | bytes 983040 | tf_op jit(solution)/shard_map/bpo,bco->bpc/dot_general | solution.py:33
  102.2 3.8 %fusion.4 = bf16[1024,512]{1,0:T(8,128)(2,1)} fusion(f32[1024,512]{1,0:T(8,128)S(1)} %fusion.123, f32[1024,512]{1,0:T(8,128)S(1)} %copy-done, f32[1024,512]{1,0:T(8,128)S(1)} %copy-done.1, f32[512,1024]{0,1:T(8,128)S(1)} %copy-done.2, f32[1024,512]{1,0:T(8,128)S(1)} %copy-done.3, f32[1024,512]{1,0:T(8,128)S(1)} %copy-done.4, f32[1024,512]{1,0:T(8,128)S(1)} %copy-done.5, ...), kind=kOutput, calls=%fused_computation.5 | convolution fusion | flops 138936320 | bytes 18219008 | tf_op jit(solution)/shard_map/bpo,bco->bpc/dot_general | solution.py:33
  106.0 1.2 fusion.160
  107.2 1.8 %copy.33 = f32[8,9,64,128]{3,2,1,0:T(8,128)} copy(f32[8,9,64,128]{3,0,2,1:T(8,128)S(1)} %bitcast.520) | data formatting | bytes 4718592
  109.0 8.1 %all-to-all-done.3 = bf16[1,9,512,128]{3,1,0,2:T(8,128)(2,1)} async-done(((bf16[1,9,512,128]{3,1,0,2:T(8,128)(2,1)}), bf16[1,9,512,128]{3,1,0,2:T(8,128)(2,1)}, u32[]{:S(2)}, u32[]{:S(2)}) %all-to-all-start.3) | async-done | bytes 1179680 | tf_op jit(solution)/shard_map/all_to_all | solution.py:48
  117.2 1.9 %copy.48 = bf16[1,9,8,64,128]{4,3,1,2,0:T(8,128)(2,1)S(1)} copy(bf16[1,9,8,64,128]{4,1,3,2,0:T(8,128)(2,1)} %bitcast.118) | data formatting | bytes 2359296 | tf_op jit(solution)/shard_map/all_to_all | solution.py:48
  119.1 0.5 reshape.868
  119.6 1.2 fusion.161
  120.8 1.8 %copy.34 = f32[8,9,64,128]{3,2,1,0:T(8,128)} copy(f32[8,9,64,128]{3,0,2,1:T(8,128)S(1)} %bitcast.521) | data formatting | bytes 4718592
  122.6 1.1 fusion.158
  123.9 1.1 fusion.159
  125.0 9.7 %all-reduce.5 = (f32[8,8]{1,0:T(8,128)S(1)}, f32[8,8]{1,0:T(8,128)S(1)}) all-reduce(f32[8,8]{1,0:T(8,128)S(1)} %fusion.158, f32[8,8]{1,0:T(8,128)S(1)} %fusion.159), channel_id=1, replica_groups=mesh['batch'=8,'chan'=4] {'chan'}, use_global_device_ids=true, to_apply=%region_1.2 | all-reduce | flops 128 | bytes 1024 | tf_op jit(solution)/shard_map/psum | solution.py:80
  134.7 10.3 %all-reduce.4 = (f32[8,8]{1,0:T(8,128)S(1)}, f32[8,8]{1,0:T(8,128)S(1)}) all-reduce(f32[8,8]{1,0:T(8,128)S(1)} %get-tuple-element.26, f32[8,8]{1,0:T(8,128)S(1)} %get-tuple-element.27), channel_id=1, replica_groups=mesh['batch'=8,'chan'=4] {'batch'}, use_global_device_ids=true, to_apply=%region_2.3 | all-reduce | flops 128 | bytes 1024 | tf_op jit(solution)/shard_map/psum | solution.py:80
  144.9 0.6 multiply_reduce_fusion.1
  145.6 0.6 multiply_reduce_fusion
  146.2 1.2 subtract_multiply_fusion.1
  147.3 1.2 subtract_multiply_fusion
  148.5 19.4 %all-reduce.9.cloned.1.call-done = (bf16[1,32,32,512]{3,2,1,0:T(8,128)(2,1)}, bf16[1,16,16,512]{3,2,1,0:T(8,128)(2,1)}) async-done(((bf16[1,32,32,512]{3,2,1,0:T(8,128)(2,1)}, bf16[1,16,16,512]{3,2,1,0:T(8,128)(2,1)}), (bf16[1,32,32,512]{3,2,1,0:T(8,128)(2,1)}, bf16[1,16,16,512]{3,2,1,0:T(8,128)(2,1)})) %all-reduce.9.cloned.1.call-update) | async-done | bytes 1310736 | tf_op jit(solution)/shard_map/psum | solution.py:45
  167.9 1.7 convert_convert_fusion
  169.6 1.5 convert_convert_fusion.1
  (63 shorter events, 3.7 us)
Async XLA Ops:
  7.2 2.1 %copy-start.20 = (f32[8,8]{1,0:T(8,128)S(1)}, f32[8,8]{1,0:T(8,128)}, u32[]{:S(2)}) copy-start(f32[8,8]{1,0:T(8,128)} %param.11) | copy-start | bytes 772
  11.6 4.4 %copy-start.8 = (bf16[8,9,64,128]{3,2,1,0:T(8,128)(2,1)S(1)}, bf16[8,9,64,128]{3,2,1,0:T(8,128)(2,1)}, u32[]{:S(2)}) copy-start(bf16[8,9,64,128]{3,2,1,0:T(8,128)(2,1)} %param.14) | copy-start | bytes 3538948
  11.6 24.0 %all-to-all-start = ((bf16[8,9,64,128]{3,2,1,0:T(8,128)(2,1)}), bf16[8,9,64,128]{3,2,1,0:T(8,128)(2,1)S(1)}, u32[]{:S(2)}, u32[]{:S(2)}) async-start(bf16[8,9,64,128]{3,2,1,0:T(8,128)(2,1)} %copy.24), calls=%async_computation | async-start | bytes 2359296 | tf_op jit(solution)/shard_map/all_to_all | solution.py:43
  16.0 1.0 copy-start.10
  16.0 1.3 copy-start.22
  21.7 0.8 copy-start.15
  21.7 1.0 copy-start.23
  23.9 0.7 copy-start.21
  29.5 1.3 copy-start.16
  29.5 1.3 copy-start.24
  31.4 3.0 %copy-start.11 = (bf16[1,32,32,128]{3,2,1,0:T(8,128)(2,1)S(1)}, bf16[1,32,32,128]{3,2,1,0:T(8,128)(2,1)}, u32[]{:S(2)}) copy-start(bf16[1,32,32,128]{3,2,1,0:T(8,128)(2,1)} %param.9) | copy-start | bytes 786436
  35.6 29.5 %all-to-all-start.1 = ((bf16[1,9,512,128]{3,1,0,2:T(8,128)(2,1)}), bf16[1,9,512,128]{3,1,0,2:T(8,128)(2,1)}, u32[]{:S(2)}, u32[]{:S(2)}) async-start(bf16[1,9,512,128]{3,1,0,2:T(8,128)(2,1)} %copy.27), calls=%async_computation.1 | async-start | bytes 4194304 | tf_op jit(solution)/shard_map/all_to_all | solution.py:48
  40.0 4.0 %copy-start.6 = (bf16[8,9,64,128]{3,2,0,1:T(8,128)(2,1)}, bf16[8,9,64,128]{3,2,0,1:T(8,128)(2,1)S(1)}, u32[]{:S(2)}) copy-start(bf16[8,9,64,128]{3,2,0,1:T(8,128)(2,1)S(1)} %copy.25) | copy-start | bytes 3538948
  65.1 21.4 %all-to-all-start.2 = ((bf16[8,9,64,128]{3,2,1,0:T(8,128)(2,1)}), bf16[8,9,64,128]{3,2,1,0:T(8,128)(2,1)}, u32[]{:S(2)}, u32[]{:S(2)}) async-start(bf16[8,9,64,128]{3,2,1,0:T(8,128)(2,1)} %copy.29), calls=%async_computation.2 | async-start | bytes 2359296 | tf_op jit(solution)/shard_map/all_to_all | solution.py:43
  75.5 2.9 %copy-start.14 = (bf16[1,32,32,128]{3,2,1,0:T(8,128)(2,1)S(1)}, bf16[1,32,32,128]{3,2,1,0:T(8,128)(2,1)}, u32[]{:S(2)}) copy-start(bf16[1,32,32,128]{3,2,1,0:T(8,128)(2,1)} %get-tuple-element.32) | copy-start | bytes 786436
  78.4 2.7 %copy-start.13 = (bf16[1,32,32,128]{3,2,1,0:T(8,128)(2,1)S(1)}, bf16[1,32,32,128]{3,2,1,0:T(8,128)(2,1)}, u32[]{:S(2)}) copy-start(bf16[1,32,32,128]{3,2,1,0:T(8,128)(2,1)} %get-tuple-element.37) | copy-start | bytes 786436
  81.1 2.7 %copy-start.12 = (bf16[1,32,32,128]{3,2,1,0:T(8,128)(2,1)S(1)}, bf16[1,32,32,128]{3,2,1,0:T(8,128)(2,1)}, u32[]{:S(2)}) copy-start(bf16[1,32,32,128]{3,2,1,0:T(8,128)(2,1)} %get-tuple-element.31) | copy-start | bytes 786436
  86.5 30.6 %all-to-all-start.3 = ((bf16[1,9,512,128]{3,1,0,2:T(8,128)(2,1)}), bf16[1,9,512,128]{3,1,0,2:T(8,128)(2,1)}, u32[]{:S(2)}, u32[]{:S(2)}) async-start(bf16[1,9,512,128]{3,1,0,2:T(8,128)(2,1)} %copy.31), calls=%async_computation.3 | async-start | bytes 4194304 | tf_op jit(solution)/shard_map/all_to_all | solution.py:48
  91.9 76.0 %all-reduce.9.cloned.1.call-start = ((), (), s32[]{:S(2)}) async-start(), calls=%async_computation.4 | async-start | bytes 2621440 | tf_op jit(solution)/shard_map/psum | solution.py:45
  91.9 10.2 %copy-start.4 = (f32[1024,512]{1,0:T(8,128)S(1)}, f32[1024,512]{1,0:T(8,128)}, u32[]{:S(2)}) copy-start(f32[1024,512]{1,0:T(8,128)} %fusion.128) | copy-start | bytes 6291460
  91.9 10.2 %copy-start.5 = (f32[1024,512]{1,0:T(8,128)S(1)}, f32[1024,512]{1,0:T(8,128)}, u32[]{:S(2)}) copy-start(f32[1024,512]{1,0:T(8,128)} %fusion.130) | copy-start | bytes 6291460
  94.6 5.1 %copy-start.19 = (bf16[1,16,16,128]{3,2,1,0:T(8,128)(2,1)S(1)}, bf16[1,16,16,128]{3,2,1,0:T(8,128)(2,1)}, u32[]{:S(2)}) copy-start(bf16[1,16,16,128]{3,2,1,0:T(8,128)(2,1)} %get-tuple-element.43) | copy-start | bytes 196612
  94.6 5.4 %copy-start.18 = (bf16[1,16,16,128]{3,2,1,0:T(8,128)(2,1)S(1)}, bf16[1,16,16,128]{3,2,1,0:T(8,128)(2,1)}, u32[]{:S(2)}) copy-start(bf16[1,16,16,128]{3,2,1,0:T(8,128)(2,1)} %get-tuple-element.44) | copy-start | bytes 196612
  95.7 2.5 %copy-start.17 = (bf16[1,16,16,128]{3,2,1,0:T(8,128)(2,1)S(1)}, bf16[1,16,16,128]{3,2,1,0:T(8,128)(2,1)}, u32[]{:S(2)}) copy-start(bf16[1,16,16,128]{3,2,1,0:T(8,128)(2,1)} %param.13) | copy-start | bytes 196612
  95.8 6.4 %copy-start.3 = (f32[1024,512]{1,0:T(8,128)S(1)}, f32[1024,512]{1,0:T(8,128)}, u32[]{:S(2)}) copy-start(f32[1024,512]{1,0:T(8,128)} %fusion.127) | copy-start | bytes 6291460
  97.0 5.2 %copy-start.2 = (f32[512,1024]{0,1:T(8,128)S(1)}, f32[512,1024]{0,1:T(8,128)}, u32[]{:S(2)}) copy-start(f32[512,1024]{0,1:T(8,128)} %fusion.126) | copy-start | bytes 6291460
  98.5 3.7 %copy-start.1 = (f32[1024,512]{1,0:T(8,128)S(1)}, f32[1024,512]{1,0:T(8,128)}, u32[]{:S(2)}) copy-start(f32[1024,512]{1,0:T(8,128)} %fusion.125) | copy-start | bytes 6291460
  100.0 2.2 %copy-start = (f32[1024,512]{1,0:T(8,128)S(1)}, f32[1024,512]{1,0:T(8,128)}, u32[]{:S(2)}) copy-start(f32[1024,512]{1,0:T(8,128)} %fusion.124) | copy-start | bytes 6291460
  120.8 1.8 %copy-start.7 = (bf16[8,9,64,128]{3,2,1,0:T(8,128)(2,1)S(1)}, bf16[8,9,64,128]{3,2,1,0:T(8,128)(2,1)}, u32[]{:S(2)}) copy-start(bf16[8,9,64,128]{3,2,1,0:T(8,128)(2,1)} %param.10) | copy-start | bytes 3538948
  122.6 1.3 copy-start.9
Sparse Core Ops, SparseCore 0:
  106.2 61.6 all-reduce.8
